TPU v7x, 512 devices: a whole 4x4x16 slice. The times are simulated.
512 devices in a mesh: dp: 64 (over y, z_hi, x, core), fsdp: 8 (over z_lo).
Axes of the slice: x: 4, y: 4, z: 16 (z_hi: 2, z_lo: 8; z = z_hi * 8 + z_lo), core: 2. Of those that a mesh axis runs over, the one named last changes fastest.
Arguments:
- inputs: bfloat16 [65536, 4096], P(('dp', 'fsdp')), may hold values from -6 to 6
- out_grad: bfloat16 [65536, 2048], P(('dp', 'fsdp')), may hold values from -24 to 24
- weight: bfloat16 [4096, 2048], P('fsdp'), may hold values from -0.125 to 0.125
- proj_basis: bfloat16 [4096, 256], P('fsdp'), may hold values from -0.09375 to 0.09375
- first_moment: float32 [64, 8192], P('dp'), may hold values from -6 to 6
- second_moment: float32 [64, 8192], P('dp'), may hold values from 0.25 to 4
Outputs:
- input_grad: bfloat16 [65536, 4096], P(('dp', 'fsdp'))
- new_first: float32 [64, 8192], P('dp')
- new_second: float32 [64, 8192], P('dp')
- update: float32 [4096, 2048], P('fsdp', 'dp')
All inputs are finite; a program needn't handle non-finite values.
Results may differ from a plain program's by a relative error of at most 0.0029.
Values may be sent and summed in bfloat16 or wider, within the bound.
No kernel may reach another device: no remote copies, remote signals or barrier semaphores. Data moves between devices by JAX's collectives and lax.ppermute only.
A program may use at most 64 MiB of HBM per device.

v0:
```python
import math
import jax
import jax.numpy as jnp
from jax import lax
from jax.sharding import PartitionSpec as P

STEP = 1000
beta_one = 0.9
beta_two = 0.999
epsilon = 1e-08


def on_device(inputs, out_grad, weight, proj_basis, first_moment, second_moment):
    tok_rows = inputs.shape[0]
    data_count = lax.axis_size("dp")
    shard_count = lax.axis_size("fsdp")
    rank_cols = proj_basis.shape[1]
    feature_grad = lax.dot_general(
        lax.all_gather(out_grad, "fsdp", axis=0, tiled=True),
        weight,
        (((1,), (1,)), ((), ())),
        preferred_element_type=jnp.float32,
    ).astype(jnp.bfloat16)
    input_grad = lax.all_to_all(feature_grad, "fsdp", split_axis=0, concat_axis=1, tiled=True)
    proj_full = jnp.dot(
        inputs,
        lax.all_gather(proj_basis, "fsdp", axis=0, tiled=True),
        preferred_element_type=jnp.float32,
    )
    projected_in = proj_full.astype(jnp.bfloat16)
    scale_factor = 1.0 / math.sqrt(tok_rows * data_count * shard_count)
    low_rank = (
        lax.dot_general(
            projected_in, out_grad, (((0,), (0,)), ((), ())), preferred_element_type=jnp.float32
        )
        * scale_factor
    )
    col_width = low_rank.shape[1] // data_count
    summed = lax.psum(low_rank, ("dp", "fsdp"))
    grad_block = lax.dynamic_slice_in_dim(summed, lax.axis_index("dp") * col_width, col_width, 1)
    flat_grad = grad_block.reshape(1, rank_cols * col_width)
    new_first = beta_one * first_moment + (1.0 - beta_one) * flat_grad
    new_second = beta_two * second_moment + (1.0 - beta_two) * flat_grad * flat_grad
    corr_one = 1.0 - beta_one**STEP
    corr_two = 1.0 - beta_two**STEP
    direction = (new_first / corr_one / (jnp.sqrt(new_second / corr_two) + epsilon)).astype(
        jnp.bfloat16
    )
    direction = direction.reshape(rank_cols, col_width)
    update = jnp.dot(proj_basis, direction, preferred_element_type=jnp.float32)
    return (input_grad, new_first, new_second, update)


def solution(mesh):
    in_specs = (
        P(("dp", "fsdp"), None),
        P(("dp", "fsdp"), None),
        P("fsdp", None),
        P("fsdp", None),
        P("dp", None),
        P("dp", None),
    )
    out_specs = (P(("dp", "fsdp"), None), P("dp", None), P("dp", None), P("fsdp", "dp"))
    return jax.shard_map(
        on_device, mesh=mesh, in_specs=in_specs, out_specs=out_specs, check_vma=False
    )
```

profile of v0, /device:TPU:1, one launch (start us, length us, event | category | flops | bytes accessed | tf_op | source)
XLA Modules:
  0.0 714.3 jit_solution(5845049301039747095)
XLA Ops:
  7.2 0.0 copy-start
  7.2 0.0 all-gather.3.cloned.1.call-start
  7.2 0.7 all-gather.3.cloned.1.call-update
  7.9 0.0 all-gather.5.cloned.1.call-start
  8.0 0.7 all-gather.5.cloned.1.call-update
  8.7 111.0 %all-gather.3.cloned.1.call-done = bf16[1024,2048]{1,0:T(8,128)(2,1)} async-done(((bf16[128,2048]{1,0:T(8,128)(2,1)}), bf16[1024,2048]{1,0:T(8,128)(2,1)}) %all-gather.3.cloned.1.call-update) | async-done | bytes 4194320 | tf_op jit(solution)/shard_map/all_gather | solution.py:19
  119.7 0.0 copy-done
  119.7 5.5 convolution_convert_fusion
  125.2 3.6 all-to-all-start
  128.8 0.0 all-reduce.2.cloned.1.call-start
  128.8 89.4 %all-gather.5.cloned.1.call-done = bf16[4096,256]{1,0:T(8,128)(2,1)} async-done(((bf16[512,256]{1,0:T(8,128)(2,1)}), bf16[4096,256]{1,0:T(8,128)(2,1)}) %all-gather.5.cloned.1.call-update) | async-done | bytes 2097168 | tf_op jit(solution)/shard_map/all_gather | solution.py:27
  218.2 4.7 convolution_multiply_fusion
  222.9 0.0 copy-start.1
  222.9 0.0 all-reduce.2.cloned.1.call-update
  222.9 478.2 %all-reduce.2.cloned.1.call-done = f32[256,2048]{0,1:T(8,128)} async-done(((f32[256,2048]{0,1:T(8,128)}), f32[256,2048]{0,1:T(8,128)}) %all-reduce.2.cloned.1.call-update) | async-done | bytes 2097168 | tf_op jit(solution)/shard_map/psum | solution.py:39
  701.2 1.4 constant_dynamic-slice_fusion
  702.5 0.9 copy.12
  703.4 0.7 reshape.53
  704.1 1.6 convert_reduce_fusion
  705.7 0.1 reshape.54
  705.8 0.0 copy-done.1
  705.8 0.8 convolution_bitcast_fusion
  706.7 0.0 all-to-all-done
  706.7 1.1 copy.13
Async XLA Ops:
  7.2 112.5 %copy-start = (bf16[512,2048]{1,0:T(8,128)(2,1)S(1)}, bf16[512,2048]{1,0:T(8,128)(2,1)}, u32[]{:S(2)}) copy-start(bf16[512,2048]{1,0:T(8,128)(2,1)} %param.8) | copy-start | bytes 6291460
  7.2 112.5 %all-gather.3.cloned.1.call-start = ((), (), s32[]{:S(2)}) async-start(), calls=%async_computation.1 | async-start | bytes 4718592 | tf_op jit(solution)/shard_map/all_gather | solution.py:19
  7.9 210.3 %all-gather.5.cloned.1.call-start = ((), (), s32[]{:S(2)}) async-start(), calls=%async_computation.2 | async-start | bytes 2359296 | tf_op jit(solution)/shard_map/all_gather | solution.py:27
  125.2 581.5 %all-to-all-start = ((bf16[8,128,512]{2,1,0:T(8,128)(2,1)}), bf16[8,128,512]{2,1,0:T(8,128)(2,1)S(1)}, u32[]{:S(2)}, u32[]{:S(2)}) async-start(bf16[8,128,512]{2,1,0:T(8,128)(2,1)} %bitcast.14), calls=%async_computation | async-start | bytes 2097152 | tf_op jit(solution)/shard_map/all_to_all | solution.py:24
  128.8 572.4 %all-reduce.2.cloned.1.call-start = ((), (), s32[]{:S(2)}) async-start(), calls=%async_computation.3 | async-start | bytes 4194304 | tf_op jit(solution)/shard_map/psum | solution.py:39
  222.9 482.9 %copy-start.1 = (bf16[512,256]{1,0:T(8,128)(2,1)S(1)}, bf16[512,256]{1,0:T(8,128)(2,1)}, u32[]{:S(2)}) copy-start(bf16[512,256]{1,0:T(8,128)(2,1)} %param.9) | copy-start | bytes 786436
Sparse Core Ops, SparseCore 0:
  10.1 109.5 all-gather.2
  121.8 96.4 all-gather.4
  223.6 477.5 all-reduce.1
where the time goes:
time: 715 us; the launch traced here: 714 us
  waiting for transfers between devices  680 us (95%)
  between operations  13.8 us (2%)
  matrix products  11 us (2%)
    psum x1, waiting for transfers between devices, on_device(): summed = lax.psum(low_rank, ('dp', 'fsdp'))  478 us
    all_gather x1, waiting for transfers between devices, on_device(): lax.all_gather(out_grad, 'fsdp', axis=0, tiled=True)  111 us
    all_gather x1, waiting for transfers between devices, on_device(): lax.all_gather(proj_basis, 'fsdp', axis=0, tiled=True)  89.4 us
  transfers between devices with their start and end apart: 4, of which 3 were waited for; matrix products, arithmetic and copies ran while one was open for 2% of the time, Pallas kernels for 0%

commit v1 on v0

--- a/solution.py
+++ b/solution.py
@@ -11,6 +11,18 @@
 
 
 def on_device(inputs, out_grad, weight, proj_basis, first_moment, second_moment):
+
+    def put_spot_all(vec, dim_i):
+        return jnp.concatenate(
+            jax.lax.all_to_all(
+                jnp.stack([vec] * jax.lax.axis_size("fsdp")),
+                axis_name="fsdp",
+                split_axis=0,
+                concat_axis=0,
+            ),
+            axis=dim_i,
+        )
+
     tok_rows = inputs.shape[0]
     data_count = lax.axis_size("dp")
     shard_count = lax.axis_size("fsdp")
@@ -22,11 +34,7 @@
         preferred_element_type=jnp.float32,
     ).astype(jnp.bfloat16)
     input_grad = lax.all_to_all(feature_grad, "fsdp", split_axis=0, concat_axis=1, tiled=True)
-    proj_full = jnp.dot(
-        inputs,
-        lax.all_gather(proj_basis, "fsdp", axis=0, tiled=True),
-        preferred_element_type=jnp.float32,
-    )
+    proj_full = jnp.dot(inputs, put_spot_all(proj_basis, 0), preferred_element_type=jnp.float32)
     projected_in = proj_full.astype(jnp.bfloat16)
     scale_factor = 1.0 / math.sqrt(tok_rows * data_count * shard_count)
     low_rank = (

time: 715 us -> 715 us (level)
  waiting for transfers between devices: 680 us -> 656 us
  starting transfers between devices: 3.68 us -> 24.4 us
    all_gather x1 -> x0, waiting for transfers between devices: 89.4 us -> none  [on_device(): lax.all_gather(proj_basis, 'fsdp', axis=0, tiled=True)]
    all_gather x1, waiting for transfers between devices: 111 us -> 168 us  [on_device(): lax.all_gather(out_grad, 'fsdp', axis=0, tiled=True)]
    all_to_all x0 -> x1, starting transfers between devices: none -> 13.1 us  [put_spot_all(): jax.lax.all_to_all(jnp.stack([vec] * jax.lax.axis_size('fsdp')), axis_nam...]
    psum x1, waiting for transfers between devices: 478 us -> 488 us  [on_device(): summed = lax.psum(low_rank, ('dp', 'fsdp'))]
    all_to_all x1, starting transfers between devices: 3.56 us -> 11.2 us  [on_device(): lax.all_to_all(feature_grad, 'fsdp', split_axis=0, concat_axis=1, tiled=T...]
  transfers between devices with their start and end apart: 4 -> 4, of which waited for: 3 -> 2; matrix products, arithmetic and copies ran while one was open for 2% -> 3% of each run, Pallas kernels for 0% -> 0%
where the time goes in v1:
time: 715 us
  waiting for transfers between devices  656 us (92%)
  starting transfers between devices  24.4 us (3%)
  between operations  15.5 us (2%)
  matrix products  11 us (2%)
    psum x1, waiting for transfers between devices, on_device(): summed = lax.psum(low_rank, ('dp', 'fsdp'))  488 us
    all_gather x1, waiting for transfers between devices, on_device(): lax.all_gather(out_grad, 'fsdp', axis=0, tiled=True)  168 us
  transfers between devices with their start and end apart: 4, of which 2 were waited for; matrix products, arithmetic and copies ran while one was open for 3% of the time, Pallas kernels for 0%

profile of v1, /device:TPU:1, one launch (start us, length us, event | category | flops | bytes accessed | tf_op | source)
XLA Modules:
  0.0 714.9 jit_solution(16595472634504363998)
XLA Ops:
  8.0 0.0 copy-start
  8.0 0.0 all-gather.2.cloned.1.call-start
  8.1 0.7 all-gather.2.cloned.1.call-update
  8.7 2.4 stack.2
  11.2 13.1 %all-to-all-start.1 = ((bf16[8,512,256]{2,1,0:T(8,128)(2,1)}), bf16[8,512,256]{2,1,0:T(8,128)(2,1)}, u32[]{:S(2)}, u32[]{:S(2)}) async-start(bf16[8,512,256]{2,1,0:T(8,128)(2,1)} %stack.2), calls=%async_computation.1 | async-start | bytes 4194304 | tf_op jit(solution)/shard_map/all_to_all | solution.py:17
  24.3 167.5 %all-gather.2.cloned.1.call-done = bf16[1024,2048]{1,0:T(8,128)(2,1)} async-done(((bf16[128,2048]{1,0:T(8,128)(2,1)}), bf16[1024,2048]{1,0:T(8,128)(2,1)}) %all-gather.2.cloned.1.call-update) | async-done | bytes 4194320 | tf_op jit(solution)/shard_map/all_gather | solution.py:31
  191.8 0.0 copy-done
  191.8 5.5 convolution_convert_fusion
  197.3 0.0 all-to-all-done.1
  197.3 11.2 %all-to-all-start = ((bf16[8,128,512]{2,1,0:T(8,128)(2,1)}), bf16[8,128,512]{2,1,0:T(8,128)(2,1)S(1)}, u32[]{:S(2)}, u32[]{:S(2)}) async-start(bf16[8,128,512]{2,1,0:T(8,128)(2,1)} %bitcast.15), calls=%async_computation | async-start | bytes 2097152 | tf_op jit(solution)/shard_map/all_to_all | solution.py:36
  208.5 0.0 all-reduce.2.cloned.1.call-start
  208.6 4.7 convolution_multiply_fusion
  213.3 0.0 copy-start.1
  213.3 0.0 all-reduce.2.cloned.1.call-update
  213.3 487.6 %all-reduce.2.cloned.1.call-done = f32[256,2048]{0,1:T(8,128)} async-done(((f32[256,2048]{0,1:T(8,128)}), f32[256,2048]{0,1:T(8,128)}) %all-reduce.2.cloned.1.call-update) | async-done | bytes 2097168 | tf_op jit(solution)/shard_map/psum | solution.py:47
  700.9 1.4 constant_dynamic-slice_fusion
  702.2 0.9 copy.12
  703.1 0.7 reshape.59
  703.8 1.6 convert_reduce_fusion
  705.4 0.1 reshape.60
  705.5 0.0 copy-done.1
  705.5 0.8 convolution_bitcast_fusion
  706.3 0.0 all-to-all-done
  706.4 1.1 copy.13
Async XLA Ops:
  8.0 183.8 %copy-start = (bf16[512,2048]{1,0:T(8,128)(2,1)S(1)}, bf16[512,2048]{1,0:T(8,128)(2,1)}, u32[]{:S(2)}) copy-start(bf16[512,2048]{1,0:T(8,128)(2,1)} %param.8) | copy-start | bytes 6291460
  8.0 183.8 %all-gather.2.cloned.1.call-start = ((), (), s32[]{:S(2)}) async-start(), calls=%async_computation.2 | async-start | bytes 4718592 | tf_op jit(solution)/shard_map/all_gather | solution.py:31
  11.2 186.1 %all-to-all-start.1 = ((bf16[8,512,256]{2,1,0:T(8,128)(2,1)}), bf16[8,512,256]{2,1,0:T(8,128)(2,1)}, u32[]{:S(2)}, u32[]{:S(2)}) async-start(bf16[8,512,256]{2,1,0:T(8,128)(2,1)} %stack.2), calls=%async_computation.1 | async-start | bytes 4194304 | tf_op jit(solution)/shard_map/all_to_all | solution.py:17
  197.3 509.0 %all-to-all-start = ((bf16[8,128,512]{2,1,0:T(8,128)(2,1)}), bf16[8,128,512]{2,1,0:T(8,128)(2,1)S(1)}, u32[]{:S(2)}, u32[]{:S(2)}) async-start(bf16[8,128,512]{2,1,0:T(8,128)(2,1)} %bitcast.15), calls=%async_computation | async-start | bytes 2097152 | tf_op jit(solution)/shard_map/all_to_all | solution.py:36
  208.5 492.3 %all-reduce.2.cloned.1.call-start = ((), (), s32[]{:S(2)}) async-start(), calls=%async_computation.3 | async-start | bytes 4194304 | tf_op jit(solution)/shard_map/psum | solution.py:47
  213.3 492.3 %copy-start.1 = (bf16[512,256]{1,0:T(8,128)(2,1)S(1)}, bf16[512,256]{1,0:T(8,128)(2,1)}, u32[]{:S(2)}) copy-start(bf16[512,256]{1,0:T(8,128)(2,1)} %param.9) | copy-start | bytes 786436
Sparse Core Ops, SparseCore 0:
  10.9 180.8 all-gather.1
Sparse Core Ops, SparseCore 1:
  214.4 486.4 all-reduce.1

commit v2 on v0

--- a/solution.py
+++ b/solution.py
@@ -3,11 +3,18 @@
 import jax.numpy as jnp
 from jax import lax
 from jax.sharding import PartitionSpec as P
+from jax.lax import psum
 
 STEP = 1000
 beta_one = 0.9
 beta_two = 0.999
 epsilon = 1e-08
+
+
+def detail_map(work_x, dev_axis, bus_axis="fsdp"):
+    for num in (dev_axis, bus_axis):
+        work_x = psum(work_x, num)
+    return work_x
 
 
 def on_device(inputs, out_grad, weight, proj_basis, first_moment, second_moment):
@@ -36,7 +43,7 @@
         * scale_factor
     )
     col_width = low_rank.shape[1] // data_count
-    summed = lax.psum(low_rank, ("dp", "fsdp"))
+    summed = detail_map(low_rank, "dp")
     grad_block = lax.dynamic_slice_in_dim(summed, lax.axis_index("dp") * col_width, col_width, 1)
     flat_grad = grad_block.reshape(1, rank_cols * col_width)
     new_first = beta_one * first_moment + (1.0 - beta_one) * flat_grad

time: 715 us -> 1440 us (2.01)
  waiting for transfers between devices: 680 us -> 1410 us
    psum x1 -> x2, waiting for transfers between devices: 478 us -> 1230 us  [detail_map(): work_x = psum(work_x, num)]
    all_gather x1, waiting for transfers between devices: 89.4 us -> 72.6 us  [on_device(): lax.all_gather(proj_basis, 'fsdp', axis=0, tiled=True)]
  transfers between devices with their start and end apart: 4 -> 5, of which waited for: 3 -> 4; matrix products, arithmetic and copies ran while one was open for 2% -> 1% of each run, Pallas kernels for 0% -> 0%
where the time goes in v2:
time: 1440 us
  waiting for transfers between devices  1410 us (98%)
    psum x2, waiting for transfers between devices, detail_map(): work_x = psum(work_x, num)  1230 us
    all_gather x1, waiting for transfers between devices, on_device(): lax.all_gather(out_grad, 'fsdp', axis=0, tiled=True)  103 us
    all_gather x1, waiting for transfers between devices, on_device(): lax.all_gather(proj_basis, 'fsdp', axis=0, tiled=True)  72.6 us
  transfers between devices with their start and end apart: 5, of which 4 were waited for; matrix products, arithmetic and copies ran while one was open for 1% of the time, Pallas kernels for 0%

profile of v2, /device:TPU:1, one launch (start us, length us, event | category | flops | bytes accessed | tf_op | source)
XLA Modules:
  0.0 1440.2 jit_solution(15756059441815510310)
XLA Ops:
  7.2 0.0 copy-start
  7.2 0.0 all-gather.5.cloned.1.call-start
  7.2 0.7 all-gather.5.cloned.1.call-update
  7.9 0.0 all-gather.3.cloned.1.call-start
  8.0 0.7 all-gather.3.cloned.1.call-update
  8.7 0.0 all-reduce.3.cloned.1.call-start
  8.7 72.6 %all-gather.5.cloned.1.call-done = bf16[4096,256]{1,0:T(8,128)(2,1)} async-done(((bf16[512,256]{1,0:T(8,128)(2,1)}), bf16[4096,256]{1,0:T(8,128)(2,1)}) %all-gather.5.cloned.1.call-update) | async-done | bytes 2097168 | tf_op jit(solution)/shard_map/all_gather | solution.py:34
  81.3 4.7 convolution_multiply_fusion
  86.0 0.0 all-reduce.3.cloned.1.call-update
  86.0 102.5 %all-gather.3.cloned.1.call-done = bf16[1024,2048]{1,0:T(8,128)(2,1)} async-done(((bf16[128,2048]{1,0:T(8,128)(2,1)}), bf16[1024,2048]{1,0:T(8,128)(2,1)}) %all-gather.3.cloned.1.call-update) | async-done | bytes 4194320 | tf_op jit(solution)/shard_map/all_gather | solution.py:26
  188.5 0.0 copy-done
  188.5 5.5 convolution_convert_fusion
  194.0 0.0 copy-start.1
  194.0 3.7 all-to-all-start
  197.7 0.0 all-reduce.5.cloned.1.call-start
  197.8 1090.3 %all-reduce.3.cloned.1.call-done = f32[256,2048]{0,1:T(8,128)} async-done(((f32[256,2048]{0,1:T(8,128)}), f32[256,2048]{0,1:T(8,128)}) %all-reduce.3.cloned.1.call-update) | async-done | bytes 2097168 | tf_op jit(solution)/shard_map/psum | solution.py:16
  1288.1 0.0 all-reduce.5.cloned.1.call-update
  1288.1 139.0 %all-reduce.5.cloned.1.call-done = f32[256,2048]{0,1:T(8,128)} async-done(((f32[256,2048]{0,1:T(8,128)}), f32[256,2048]{0,1:T(8,128)}) %all-reduce.5.cloned.1.call-update) | async-done | bytes 2097168 | tf_op jit(solution)/shard_map/psum | solution.py:16
  1427.1 1.4 constant_dynamic-slice_fusion
  1428.5 0.9 copy.12
  1429.3 0.7 reshape.53
  1430.0 1.6 convert_reduce_fusion
  1431.7 0.1 reshape.54
  1431.7 0.0 copy-done.1
  1431.8 0.8 convolution_bitcast_fusion
  1432.6 0.0 all-to-all-done
  1432.6 1.1 copy.13
Async XLA Ops:
  7.2 181.3 %copy-start = (bf16[512,2048]{1,0:T(8,128)(2,1)S(1)}, bf16[512,2048]{1,0:T(8,128)(2,1)}, u32[]{:S(2)}) copy-start(bf16[512,2048]{1,0:T(8,128)(2,1)} %param.8) | copy-start | bytes 6291460
  7.2 74.1 %all-gather.5.cloned.1.call-start = ((), (), s32[]{:S(2)}) async-start(), calls=%async_computation.2 | async-start | bytes 2359296 | tf_op jit(solution)/shard_map/all_gather | solution.py:34
  7.9 180.6 %all-gather.3.cloned.1.call-start = ((), (), s32[]{:S(2)}) async-start(), calls=%async_computation.1 | async-start | bytes 4718592 | tf_op jit(solution)/shard_map/all_gather | solution.py:26
  8.7 1279.4 %all-reduce.3.cloned.1.call-start = ((), (), s32[]{:S(2)}) async-start(), calls=%async_computation.3 | async-start | bytes 4194304 | tf_op jit(solution)/shard_map/psum | solution.py:16
  194.0 1237.7 %copy-start.1 = (bf16[512,256]{1,0:T(8,128)(2,1)S(1)}, bf16[512,256]{1,0:T(8,128)(2,1)}, u32[]{:S(2)}) copy-start(bf16[512,256]{1,0:T(8,128)(2,1)} %param.9) | copy-start | bytes 786436
  194.0 1238.6 %all-to-all-start = ((bf16[8,128,512]{2,1,0:T(8,128)(2,1)}), bf16[8,128,512]{2,1,0:T(8,128)(2,1)S(1)}, u32[]{:S(2)}, u32[]{:S(2)}) async-start(bf16[8,128,512]{2,1,0:T(8,128)(2,1)} %bitcast.14), calls=%async_computation | async-start | bytes 2097152 | tf_op jit(solution)/shard_map/all_to_all | solution.py:31
  197.7 1229.4 %all-reduce.5.cloned.1.call-start = ((), (), s32[]{:S(2)}) async-start(), calls=%async_computation.4 | async-start | bytes 4194304 | tf_op jit(solution)/shard_map/psum | solution.py:16
Sparse Core Ops, SparseCore 0:
  10.1 71.1 all-gather.4
  83.3 105.0 all-gather.2
  191.4 1096.6 all-reduce.2
  1291.1 135.8 all-reduce.4
